TPU v7x, 256 devices: a whole 4x4x8 slice. The times are simulated.
256 devices in a mesh: seq: 8 (over y_lo, x), chan: 32 (over y_hi, z, core).
Axes of the slice: x: 4, y: 4 (y_hi: 2, y_lo: 2; y = y_hi * 2 + y_lo), z: 8, core: 2. Of those that a mesh axis runs over, the one named last changes fastest.
Arguments:
- query_in: bfloat16 [2048, 4096], P('seq', 'chan'), may hold values from -6 to 6
- key_in: bfloat16 [2048, 4096], P('seq', 'chan'), may hold values from -6 to 6
- value_in: bfloat16 [2048, 4096], P('seq', 'chan'), may hold values from -6 to 6
- filter_taps: bfloat16 [256, 2048], P('chan', 'seq'), may hold values from -1.05 to 1.05, as said below
- skip_gain: float32 [4096], P('chan'), may hold values from 0.5 to 1.5
- out_weight: bfloat16 [4096, 4096], P('chan'), may hold values from -0.09375 to 0.09375
Outputs:
- mixed_out: bfloat16 [2048, 4096], P('seq', 'chan')
Inputs may be any that keep to these rules, and one draw needn't show every extreme that they name: `filter_taps`: taps of every filter; the filters differ in how fast their taps fade with the lag.
All inputs are finite; a program needn't handle non-finite values.
Results may differ from a plain program's by a relative error of at most 0.0057.
Values may be sent and summed in bfloat16 or wider, within the bound.
A program may use at most 64 MiB of HBM per device.

v0:
```python
import math

import jax
import jax.numpy as jnp
from jax import lax
from jax.sharding import PartitionSpec as P


def window_matrix(window, tile_size):
    reversed_window = window[:, ::-1]
    extended = jnp.concatenate(
        [reversed_window, jnp.zeros((window.shape[0], 1), window.dtype)], axis=1
    )
    repeated = jnp.tile(extended, (1, tile_size))[:, : tile_size * (2 * tile_size - 1)]
    return repeated.reshape(window.shape[0], tile_size, 2 * tile_size - 1)[:, :, tile_size - 1 :]


def accumulate(running, segment, tap_table, own_start):
    row_count, chan_width = running.shape
    group_count = tap_table.shape[0]
    tap_span = tap_table.shape[1] // 2
    group_width = chan_width // group_count
    block_rows = min(segment.shape[0], row_count)
    tile_size = math.gcd(math.gcd(block_rows, row_count), 128)
    out_tiles = row_count // tile_size
    in_tiles = block_rows // tile_size

    def one_block(step_index, current):
        block_start = step_index * block_rows
        in_blocks = lax.dynamic_slice_in_dim(segment, step_index * block_rows, block_rows, 0)
        in_blocks = in_blocks.reshape(in_tiles, tile_size, group_count, group_width)

        def add_block(previous):
            out_blocks = previous.reshape(out_tiles, tile_size, group_count, group_width)
            offset = own_start - block_start
            for lag_step in range(1 - in_tiles, out_tiles):
                tap_first = offset + lag_step * tile_size - (tile_size - 1) + tap_span
                window = lax.dynamic_slice_in_dim(tap_table, tap_first, 2 * tile_size - 1, 1)
                matrix = window_matrix(window, tile_size)
                first_out = max(0, lag_step)
                last_out = min(out_tiles, in_tiles + lag_step)
                addend = jnp.einsum(
                    "gij,qjgc->qigc",
                    matrix,
                    in_blocks[first_out - lag_step : last_out - lag_step],
                    preferred_element_type=jnp.float32,
                )
                out_blocks = out_blocks.at[first_out:last_out].add(addend)
            return out_blocks.reshape(previous.shape)

        def keep_same(previous):
            return previous

        needed = (block_start < own_start + row_count) & (block_start >= 0)
        return lax.cond(needed, add_block, keep_same, current)

    return lax.fori_loop(0, segment.shape[0] // block_rows, one_block, running)


def body(query_in, key_in, value_in, filter_taps, skip_gain, out_weight):
    row_count, chan_width = query_in.shape
    mixed_in = (key_in.astype(jnp.float32) * value_in.astype(jnp.float32)).astype(jnp.bfloat16)
    all_taps = lax.all_gather(filter_taps, "seq", axis=1, tiled=True)
    tap_table = jnp.concatenate([jnp.zeros_like(all_taps), all_taps], axis=1)
    seq_index = lax.axis_index("seq")
    own_start = seq_index * row_count
    zero_sum = jnp.zeros((row_count, chan_width), jnp.float32)
    convolved = accumulate(
        zero_sum, lax.all_gather(mixed_in, "seq", axis=0, tiled=True), tap_table, own_start
    )
    gated = (
        query_in.astype(jnp.float32)
        * (convolved + skip_gain[None, :] * mixed_in.astype(jnp.float32))
    ).astype(jnp.bfloat16)
    result = lax.psum_scatter(
        lax.dot_general(
            out_weight, gated, (((0,), (1,)), ((), ())), preferred_element_type=jnp.float32
        ),
        "chan",
        scatter_dimension=0,
        tiled=True,
    )
    return result.T.astype(jnp.bfloat16)


def solution(mesh):
    placed = (
        P("seq", "chan"),
        P("seq", "chan"),
        P("seq", "chan"),
        P("chan", "seq"),
        P("chan"),
        P("chan", None),
    )
    return jax.shard_map(
        body, mesh=mesh, in_specs=placed, out_specs=P("seq", "chan"), check_vma=False
    )
```

profile of v0, /device:TPU:1, one launch (start us, length us, event | category | flops | bytes accessed | tf_op | source)
XLA Modules:
  0.0 257.5 jit_solution(13386952036557591478)
XLA Ops:
  6.5 0.0 copy-start
  6.5 0.0 reduce-scatter.2.cloned.1.call-start
  6.5 23.4 %all_gather.7 = bf16[8,2048]{1,0:T(8,128)(2,1)S(1)} all-gather(bf16[8,256]{1,0:T(8,128)(2,1)} %param.21), channel_id=1, replica_groups=mesh['seq'=8,'chan'=32] {'seq'}, dimensions={1}, use_global_device_ids=true | all-gather | bytes 36864 | tf_op jit(solution)/shard_map/all_gather | solution.py:63
  30.0 0.9 copy.14
  30.9 0.9 copy.15
  31.9 0.9 copy.16
  32.8 22.8 %all_gather.6 = bf16[2048,128]{0,1:T(8,128)(2,1)S(1)} all-gather(bf16[256,128]{0,1:T(8,128)(2,1)S(1)} %multiply_convert_fusion.1), channel_id=1, replica_groups=mesh['seq'=8,'chan'=32] {'seq'}, dimensions={0}, use_global_device_ids=true | all-gather | bytes 589824 | tf_op jit(solution)/shard_map/all_gather | solution.py:69
  55.7 0.0 copy-start.1
  55.7 6.9 %while.21 = (s32[]{:T(128)}, f32[256,128]{0,1:T(8,128)S(1)}, s32[]{:T(128)}, bf16[2048,128]{0,1:T(8,128)(2,1)S(1)}, s32[]{:T(128)}, /*index=5*/bf16[8,4096]{1,0:T(8,128)(2,1)S(1)}, s32[]{:T(128)}, s32[]{:T(128)}, s32[]{:T(128)}) while((s32[]{:T(128)}, f32[256,128]{0,1:T(8,128)S(1)}, s32[]{:T(128)}, bf16[2048,128]{0,1:T(8,128)(2,1)S(1)}, ...), condition=%wide.region_3.4_spmd, body=%wide.region_0.3_spmd.sunk | while | flops 16842776 | bytes 11358373 | solution.py:57
  55.7 6.6 %conditional.2 = (f32[256,128]{0,1:T(8,128)S(1)}) conditional(s32[]{:T(128)} %convert_element_type.51, f32[256,128]{0,1:T(8,128)S(1)} %get-tuple-element.297, (f32[256,128]{0,1:T(8,128)S(1)}, s32[]{:T(128)}, bf16[2048,128]{0,1:T(8,128)(2,1)S(1)}, s32[]{:T(128)}, bf16[8,4096]{1,0:T(8,128)(2,1)S(1)}) %tuple.67), branch_computations={%region_1.0_spmd, %region_2.2_spmd} | conditional | flops 16842768 | bytes 11358202 | solution.py:55
  55.8 0.1 constant_dynamic-slice_fusion.2
  55.9 0.2 reverse.2
  56.0 0.1 slice.137
  56.1 0.2 reverse.1
  56.3 0.1 slice.136
  56.4 0.2 reverse
  56.5 0.1 slice.135
  56.7 0.1 reshape.171
  56.9 1.4 reshape.174
  58.3 0.3 fusion.4
  58.7 1.4 reshape.176
  60.1 0.3 fusion.6
  60.5 1.4 reshape.179
  61.9 0.3 fusion.1
  62.2 0.1 copy.13
  62.6 0.0 copy-done
  62.6 0.0 copy-done.1
  62.6 2.7 %convolution_bitcast_fusion.2 = f32[4096,256]{0,1:T(8,128)} fusion(bf16[128,4096]{1,0:T(8,128)(2,1)S(1)} %copy-done, f32[256,128]{0,1:T(8,128)S(1)} %get-tuple-element.221, bf16[256,128]{0,1:T(8,128)(2,1)S(1)} %multiply_convert_fusion.1, bf16[256,128]{0,1:T(8,128)(2,1)S(1)} %copy.14, f32[128]{0:T(128)S(1)} %copy-done.1), kind=kOutput, calls=%fused_computation.18 | convolution fusion | flops 268632064 | bytes 5505536 | tf_op jit(solution)/shard_map/dot_general | solution.py:76
  65.4 0.0 reduce-scatter.2.cloned.1.call-update
  65.4 183.7 %reduce-scatter.2.cloned.1.call-done = f32[128,256]{0,1:T(8,128)} async-done(((f32[4096,256]{0,1:T(8,128)}), f32[128,256]{0,1:T(8,128)}) %reduce-scatter.2.cloned.1.call-update) | async-done | bytes 131088 | tf_op jit(solution)/shard_map/reduce_scatter | solution.py:75
  249.1 1.5 convert_bitcast_fusion
  (27 shorter events, 0.5 us)
Async XLA Ops:
  6.5 56.1 %copy-start = (bf16[128,4096]{1,0:T(8,128)(2,1)S(1)}, bf16[128,4096]{1,0:T(8,128)(2,1)}, u32[]{:S(2)}) copy-start(bf16[128,4096]{1,0:T(8,128)(2,1)} %param.23) | copy-start | bytes 3145732
  6.5 242.6 %reduce-scatter.2.cloned.1.call-start = ((), (), s32[]{:S(2)}) async-start(), calls=%async_computation.1 | async-start | bytes 4325376 | tf_op jit(solution)/shard_map/reduce_scatter | solution.py:75
  55.7 6.9 %copy-start.1 = (f32[128]{0:T(128)S(1)}, f32[128]{0:T(128)}, u32[]{:S(2)}) copy-start(f32[128]{0:T(128)} %param.22) | copy-start | bytes 1540
Sparse Core Ops, SparseCore 0:
  65.5 183.5 reduce-scatter.1
where the time goes:
time: 262 us; the launch traced here: 258 us
  waiting for transfers between devices  184 us (70%)
  blocking collectives  46.3 us (18%)
  between operations  13.5 us (5%)
  local copies, waits for them, and re-layouts  8.27 us (3%)
  matrix products  3.67 us (1%)
    reduce_scatter x1, waiting for transfers between devices, body(): lax.psum_scatter(lax.dot_general(out_weight, gated, (((0,), (1,)), ((), (...  184 us
    all_gather x1, blocking collectives, body(): all_taps = lax.all_gather(filter_taps, 'seq', axis=1, tiled=True)  23.4 us
    all_gather x1, blocking collectives, body(): lax.all_gather(mixed_in, 'seq', axis=0, tiled=True)  22.8 us
  transfers between devices with their start and end apart: 1, of which 1 were waited for; matrix products, arithmetic and copies ran while one was open for 0% of the time, Pallas kernels for 0%

commit v1 on v0

v1 whole, which is shorter than its diff:
```python
import functools

import jax
import jax.numpy as jnp
from jax import lax
from jax.experimental import pallas as pl
from jax.experimental.pallas import tpu as pltpu
from jax.sharding import PartitionSpec as P

MESH = pl.DeviceIdType.MESH
BF = jnp.bfloat16
F32 = jnp.float32
SEQ = 8
RING = 8
ROWS = 256
WIDTH = 128
GROUP = 16
HALF = 128
CHUNKS = 4
PIECE = HALF // CHUNKS


def aligned(value, multiple):
    return pl.multiple_of(value, multiple)


def wait_bytes(ref, sem):
    pltpu.make_async_copy(ref, ref, sem).wait()


def kernel(
    q_hbm, k_hbm, v_hbm, taps_hbm, gain_hbm, w_hbm, out_ref,
    q_in, k_in, v_in, gain, wbuf,
    m_send, q_send, m_recv, q_recv, taps_recv, tmat, conv, g_send, g_recv, g_rows,
    part_a, part_b,
    sa_up, ra_up, sa_dn, ra_dn, sa_y, ra_y,
    sb_y, rb_y, sb_up, rb_up, sb_dn, rb_dn,
    load_sem, w_sem, w_rs, a2a_sem,
    a_up_sem, a_dn_sem, a_y_sem, b_y_sem, b_up_sem, b_dn_sem, send_sem,
):
    s = lax.axis_index("seq")
    k = lax.axis_index("chan")
    core = k % 2
    z = (k // 2) % RING
    yh = k // (2 * RING)
    mate = k + 1 - 2 * core
    up = yh * (2 * RING) + ((z + 1) % RING) * 2 + core
    down = yh * (2 * RING) + ((z + RING - 1) % RING) * 2 + core
    across = (1 - yh) * (2 * RING) + z * 2 + core

    loads = [
        pltpu.make_async_copy(k_hbm, k_in, load_sem.at[0]),
        pltpu.make_async_copy(v_hbm, v_in, load_sem.at[1]),
        pltpu.make_async_copy(q_hbm, q_in, load_sem.at[2]),
        pltpu.make_async_copy(gain_hbm, gain, load_sem.at[3]),
        pltpu.make_async_copy(taps_hbm, taps_recv.at[s], load_sem.at[4]),
    ]
    for load in loads:
        load.start()

    barrier = pltpu.get_barrier_semaphore()
    greeted = [((s + i) % SEQ, c) for i in range(1, SEQ) for c in (k, mate)]
    greeted += [(s, mate), (s, up), (s, down), (s, across)]
    for target in greeted:
        pl.semaphore_signal(barrier, inc=1, device_id=target, device_id_type=MESH)

    def slot_col(r, yr, c):
        block = ((yh + yr) % 2) * (2 * RING) + ((z + r) % RING) * 2 + c
        return aligned(block * WIDTH, WIDTH)

    own_rows = pl.ds(aligned(core * WIDTH, WIDTH), WIDTH)
    for r in range(RING):
        for yr in range(2):
            slot = pl.ds((2 * r + yr) * WIDTH, WIDTH)
            pltpu.make_async_copy(
                w_hbm.at[:, pl.ds(slot_col(r, yr, core), WIDTH)], wbuf.at[own_rows, slot], w_sem
            ).start()

    loads[0].wait()
    loads[1].wait()
    mixed = (k_in[...].astype(F32) * v_in[...].astype(F32)).astype(BF)
    m_send[...] = mixed.astype(F32).T.astype(BF)
    loads[2].wait()
    q_send[...] = q_in[...].astype(F32).T.astype(BF)
    mine = pl.ds(aligned(s * GROUP, GROUP), GROUP)
    m_recv[mine, :] = m_send[mine, :]
    q_recv[mine, :] = q_send[mine, :]
    loads[3].wait()
    loads[4].wait()

    pl.semaphore_wait(barrier, len(greeted))

    peers = [(s + i) % SEQ for i in range(1, SEQ)]

    def remote(src, dst, send, recv, target):
        copy = pltpu.make_async_remote_copy(
            src_ref=src, dst_ref=dst, send_sem=send, recv_sem=recv,
            device_id=target, device_id_type=MESH,
        )
        copy.start()
        return copy

    for p in peers:
        remote(taps_hbm, taps_recv.at[s], send_sem.at[0], a2a_sem.at[0], (p, k))
    for p in peers:
        rows = pl.ds(aligned(p * GROUP, GROUP), GROUP)
        remote(m_send.at[rows, :], m_recv.at[mine, :], send_sem.at[1], a2a_sem.at[1], (p, k))
    for p in peers:
        rows = pl.ds(aligned(p * GROUP, GROUP), GROUP)
        remote(q_send.at[rows, :], q_recv.at[mine, :], send_sem.at[2], a2a_sem.at[2], (p, k))
    for r in range(RING):
        for yr in range(2):
            slot = pl.ds((2 * r + yr) * WIDTH, WIDTH)
            remote(
                w_hbm.at[:, pl.ds(slot_col(r, yr, 1 - core), WIDTH)], wbuf.at[own_rows, slot],
                send_sem.at[3], w_rs, (s, mate),
            )

    wait_bytes(taps_recv.at[pl.ds(0, SEQ - 1)], a2a_sem.at[0])
    all_taps = taps_recv[...].astype(F32)
    group_row = lax.broadcasted_iota(jnp.int32, all_taps.shape, 1)
    taps = jnp.sum(jnp.where(group_row == s, all_taps, 0.0), axis=1)
    row = lax.broadcasted_iota(jnp.int32, (ROWS, ROWS), 0)
    col = lax.broadcasted_iota(jnp.int32, (ROWS, ROWS), 1)
    upper = col >= row
    before = jnp.zeros((ROWS, ROWS), F32)
    for d in range(SEQ):
        spread = jnp.broadcast_to(taps[d : d + 1, :], (ROWS, ROWS))
        rolled = pltpu.roll(spread, 0, 1, stride=1, stride_axis=0)
        tmat[d] = jnp.where(upper, rolled, before).astype(BF)
        before = rolled

    lane = lax.broadcasted_iota(jnp.int32, (WIDTH, WIDTH), 1)
    line = lax.broadcasted_iota(jnp.int32, (WIDTH, WIDTH), 0)
    picked = jnp.where(lane == s * GROUP + line % GROUP, jnp.broadcast_to(gain[...], (WIDTH, WIDTH)), 0.0)
    row_gain = jnp.sum(picked, axis=1, keepdims=True)

    wait_bytes(m_recv.at[pl.ds(0, GROUP * (SEQ - 1)), :], a2a_sem.at[1])
    conv[...] = jnp.dot(m_recv[...], tmat[0], preferred_element_type=F32)
    for d in range(1, SEQ):
        kept = WIDTH - GROUP * d
        conv[GROUP * d :, :] += jnp.dot(m_recv[:kept, :], tmat[d], preferred_element_type=F32)
    wait_bytes(q_recv.at[pl.ds(0, GROUP * (SEQ - 1)), :], a2a_sem.at[2])
    gated = q_recv[...].astype(F32) * (conv[...] + row_gain * m_recv[...].astype(F32))
    g_send[...] = gated.astype(BF)

    land = pl.ds(aligned(core * WIDTH + s * GROUP, GROUP), GROUP)
    for p in peers:
        rows = pl.ds(aligned(p * GROUP, GROUP), GROUP)
        for c in (k, mate):
            remote(g_send.at[rows, :], g_recv.at[land, :], send_sem.at[4], a2a_sem.at[3], (p, c))
    remote(g_send.at[mine, :], g_recv.at[land, :], send_sem.at[4], a2a_sem.at[3], (s, mate))
    g_recv[land, :] = g_send[mine, :]

    wait_bytes(wbuf.at[pl.ds(0, WIDTH), :], w_sem)
    wait_bytes(wbuf.at[pl.ds(0, WIDTH), :], w_rs)
    wait_bytes(g_recv.at[pl.ds(0, 2 * WIDTH - GROUP), :], a2a_sem.at[3])
    g_rows[...] = g_recv[...].astype(F32).T.astype(BF)

    def product(first, r):
        return jnp.dot(
            g_rows[first : first + HALF, :], wbuf[:, 2 * r * WIDTH : 2 * (r + 1) * WIDTH],
            preferred_element_type=F32,
        )

    def piece(c):
        return pl.ds(c * PIECE, PIECE)

    def hop(send, recv, sems, group, step, c, target):
        return remote(
            send.at[step, piece(c), :], recv.at[step, piece(c), :],
            send_sem.at[group], sems.at[step * CHUNKS + c], target,
        )

    def arrive(recv, sems, step, c):
        wait_bytes(recv.at[step, piece(c), :], sems.at[step * CHUNKS + c])
        return recv[step, piece(c), :].astype(F32)

    sa_up[0] = product(0, 4).astype(BF)
    for c in range(CHUNKS):
        hop(sa_up, ra_up, a_up_sem, 5, 0, c, (s, up))
    sa_dn[0] = product(0, 5).astype(BF)
    for c in range(CHUNKS):
        hop(sa_dn, ra_dn, a_dn_sem, 6, 0, c, (s, down))
    order = (4, 3, 5, 2, 6, 1, 7, 0)
    for r in order:
        both = product(HALF, r)
        part_b[r] = both[:, :WIDTH]
        sb_y[r] = both[:, WIDTH:].astype(BF)
        remote(sb_y.at[r], rb_y.at[r], send_sem.at[7], b_y_sem.at[r], (s, across))
    for r in (3, 6, 2, 7, 1, 0):
        part_a[r] = product(0, r)

    def a_step(t):
        for c in range(CHUNKS):
            if t <= 3:
                got = arrive(ra_up, a_up_sem, t - 1, c)
                sa_up[t, piece(c), :] = (part_a[4 - t, piece(c), :] + got).astype(BF)
                hop(sa_up, ra_up, a_up_sem, 5, t, c, (s, up))
            if t <= 2:
                got = arrive(ra_dn, a_dn_sem, t - 1, c)
                sa_dn[t, piece(c), :] = (part_a[5 + t, piece(c), :] + got).astype(BF)
                hop(sa_dn, ra_dn, a_dn_sem, 6, t, c, (s, down))

    def b_own(r):
        wait_bytes(rb_y.at[r], b_y_sem.at[r])
        part_b[r] = part_b[r] + rb_y[r].astype(F32)

    def b_step(t):
        b_own(4 + t)
        if t <= 2:
            b_own(3 - t)
        for c in range(CHUNKS):
            value = part_b[4 + t, piece(c), :]
            if t > 0:
                value = value + arrive(rb_dn, b_dn_sem, t - 1, c)
            sb_dn[t, piece(c), :] = value.astype(BF)
            hop(sb_dn, rb_dn, b_dn_sem, 8, t, c, (s, down))
            if t <= 2:
                value = part_b[3 - t, piece(c), :]
                if t > 0:
                    value = value + arrive(rb_up, b_up_sem, t - 1, c)
                sb_up[t, piece(c), :] = value.astype(BF)
                hop(sb_up, rb_up, b_up_sem, 9, t, c, (s, up))

    a_step(1)
    b_step(0)
    a_step(2)
    b_step(1)
    a_step(3)
    b_step(2)
    for c in range(CHUNKS):
        total = part_a[0, piece(c), :] + arrive(ra_dn, a_dn_sem, 2, c) + arrive(ra_up, a_up_sem, 3, c)
        part_a[0, piece(c), :] = total
        sa_y[piece(c), :] = total[:, WIDTH:].astype(BF)
        remote(sa_y.at[piece(c), :], ra_y.at[piece(c), :], send_sem.at[10], a_y_sem.at[c], (s, across))
    b_step(3)
    b_own(0)
    for c in range(CHUNKS):
        total = part_b[0, piece(c), :] + arrive(rb_up, b_up_sem, 2, c) + arrive(rb_dn, b_dn_sem, 3, c)
        out_ref[pl.ds(HALF + c * PIECE, PIECE), :] = total.astype(BF)
    for c in range(CHUNKS):
        wait_bytes(ra_y.at[piece(c), :], a_y_sem.at[c])
        total = part_a[0, piece(c), :WIDTH] + ra_y[piece(c), :].astype(F32)
        out_ref[piece(c), :] = total.astype(BF)

    wait_bytes(taps_recv.at[pl.ds(0, SEQ - 1)], send_sem.at[0])
    wait_bytes(m_recv.at[pl.ds(0, GROUP * (SEQ - 1)), :], send_sem.at[1])
    wait_bytes(q_recv.at[pl.ds(0, GROUP * (SEQ - 1)), :], send_sem.at[2])
    wait_bytes(wbuf.at[pl.ds(0, WIDTH), :], send_sem.at[3])
    wait_bytes(g_recv.at[pl.ds(0, 2 * WIDTH - GROUP), :], send_sem.at[4])
    wait_bytes(sa_up, send_sem.at[5])
    wait_bytes(sa_dn, send_sem.at[6])
    wait_bytes(sb_y, send_sem.at[7])
    wait_bytes(sb_dn, send_sem.at[8])
    wait_bytes(sb_up, send_sem.at[9])
    wait_bytes(sa_y, send_sem.at[10])


def body(query_in, key_in, value_in, filter_taps, skip_gain, out_weight):
    dma = pltpu.SemaphoreType.DMA
    hbm = pl.BlockSpec(memory_space=pltpu.MemorySpace.HBM)
    return pl.pallas_call(
        kernel,
        out_shape=jax.ShapeDtypeStruct((ROWS, WIDTH), BF),
        in_specs=[hbm] * 6,
        out_specs=pl.BlockSpec(memory_space=pltpu.VMEM),
        scratch_shapes=[
            pltpu.VMEM((ROWS, WIDTH), BF),
            pltpu.VMEM((ROWS, WIDTH), BF),
            pltpu.VMEM((ROWS, WIDTH), BF),
            pltpu.VMEM((1, WIDTH), F32),
            pltpu.VMEM((2 * WIDTH, 2 * RING * WIDTH), BF),
            pltpu.VMEM((WIDTH, ROWS), BF),
            pltpu.VMEM((WIDTH, ROWS), BF),
            pltpu.VMEM((WIDTH, ROWS), BF),
            pltpu.VMEM((WIDTH, ROWS), BF),
            pltpu.VMEM((SEQ, SEQ, ROWS), BF),
            pltpu.VMEM((SEQ, ROWS, ROWS), BF),
            pltpu.VMEM((WIDTH, ROWS), F32),
            pltpu.VMEM((WIDTH, ROWS), BF),
            pltpu.VMEM((2 * WIDTH, ROWS), BF),
            pltpu.VMEM((ROWS, 2 * WIDTH), BF),
            pltpu.VMEM((RING, HALF, 2 * WIDTH), F32),
            pltpu.VMEM((RING, HALF, WIDTH), F32),
            pltpu.VMEM((4, HALF, 2 * WIDTH), BF),
            pltpu.VMEM((4, HALF, 2 * WIDTH), BF),
            pltpu.VMEM((3, HALF, 2 * WIDTH), BF),
            pltpu.VMEM((3, HALF, 2 * WIDTH), BF),
            pltpu.VMEM((HALF, WIDTH), BF),
            pltpu.VMEM((HALF, WIDTH), BF),
            pltpu.VMEM((RING, HALF, WIDTH), BF),
            pltpu.VMEM((RING, HALF, WIDTH), BF),
            pltpu.VMEM((3, HALF, WIDTH), BF),
            pltpu.VMEM((3, HALF, WIDTH), BF),
            pltpu.VMEM((4, HALF, WIDTH), BF),
            pltpu.VMEM((4, HALF, WIDTH), BF),
            dma((5,)),
            dma,
            dma,
            dma((4,)),
            dma((4 * CHUNKS,)),
            dma((3 * CHUNKS,)),
            dma((CHUNKS,)),
            dma((RING,)),
            dma((3 * CHUNKS,)),
            dma((4 * CHUNKS,)),
            dma((11,)),
        ],
        compiler_params=pltpu.CompilerParams(collective_id=0, has_side_effects=True),
    )(query_in, key_in, value_in, filter_taps, skip_gain.reshape(1, WIDTH), out_weight)


def solution(mesh):
    placed = (
        P("seq", "chan"),
        P("seq", "chan"),
        P("seq", "chan"),
        P("chan", "seq"),
        P("chan"),
        P("chan", None),
    )
    return jax.shard_map(
        body, mesh=mesh, in_specs=placed, out_specs=P("seq", "chan"), check_vma=False
    )
```

time: 262 us -> 38.1 us (0.15)
  the two profiles are of different devices: /device:TPU:1 before, /device:TPU:64 now
where the time goes in v1:
time: 38.1 us; the launch traced here: 37.9 us
  Pallas kernels  36.4 us (96%)
  local copies, waits for them, and re-layouts  1.47 us (4%)
    pallas_call x1, Pallas kernels, body(): pl.pallas_call(kernel, out_shape=jax.ShapeDtypeStruct((ROWS, WIDTH), BF),...  36.4 us
    unnamed x1, local copies, waits for them, and re-layouts  1.47 us

profile of v1, /device:TPU:64, one launch (start us, length us, event | category | flops | bytes accessed | tf_op | source)
XLA Modules:
  0.0 37.9 jit_solution(11930231426568960453)
XLA Ops:
  0.0 36.4 %shard_map.64 = bf16[256,128]{1,0:T(8,128)(2,1)} custom-call(bf16[256,128]{1,0:T(8,128)(2,1)} %q_hbm.1, bf16[256,128]{1,0:T(8,128)(2,1)} %k_hbm.1, bf16[256,128]{1,0:T(8,128)(2,1)} %v_hbm.1, bf16[8,256]{1,0:T(8,128)(2,1)} %taps_hbm.1, f32[1,128]{1,0:T(1,128)} %bitcast.1, bf16[128,4096]{1,0:T(8,128)(2,1)} %w_hbm.1), custom_call_target="tpu_custom_call" | custom-call | tf_op jit(solution)/shard_map/pallas_call | solution.py:263
  36.4 1.5 %copy.8 = bf16[256,128]{1,0:T(8,128)(2,1)} copy(bf16[256,128]{1,0:T(8,128)(2,1)} %shard_map.64) | data formatting | bytes 131072

commit v2 on v1

v2 whole, which is shorter than its diff:
```python
import functools

import jax
import jax.numpy as jnp
from jax import lax
from jax.experimental import pallas as pl
from jax.experimental.pallas import tpu as pltpu
from jax.sharding import PartitionSpec as P

MESH = pl.DeviceIdType.MESH
BF = jnp.bfloat16
F32 = jnp.float32
SEQ = 8
RING = 8
ROWS = 256
WIDTH = 128
GROUP = 16
HALF = 128
PLACES = (4, 3, 5, 1, 7, 2, 6, 0)
PAIRS = 4
FIRST_PAIRS = 2
R4, UP3, DOWN3, UP1, DOWN1, UP2, DOWN2 = range(7)


def aligned(value, multiple):
    return pl.multiple_of(value, multiple)


def wait_bytes(ref, sem):
    pltpu.make_async_copy(ref, ref, sem).wait()


def kernel(
    q_hbm, k_hbm, v_hbm, taps_hbm, gain_hbm, w_hbm, out_ref,
    q_in, k_in, v_in, gain, wbuf,
    m_send, q_send, m_recv, q_recv, taps_recv, tmat, conv, g_send, g_recv, g_rows,
    part, out_send, out_recv,
    load_sem, w_near, w_far, a2a_sem, g_sem, out_sem, send_sem,
):
    s = lax.axis_index("seq")
    k = lax.axis_index("chan")
    core = k % 2
    z = (k // 2) % RING
    yh = k // (2 * RING)

    def chan(y, level, c):
        return y * (2 * RING) + ((level + RING) % RING) * 2 + c

    mate = chan(yh, z, 1 - core)
    sharing = [chan(y, z, c) for y in (yh, 1 - yh) for c in (core, 1 - core)]
    near = (s + SEQ // 2) % SEQ
    far_rows = [(near, chan(1 - yh, z, c), c) for c in (core, 1 - core)]

    loads = [
        pltpu.make_async_copy(k_hbm, k_in, load_sem.at[0]),
        pltpu.make_async_copy(v_hbm, v_in, load_sem.at[1]),
        pltpu.make_async_copy(q_hbm, q_in, load_sem.at[2]),
        pltpu.make_async_copy(gain_hbm, gain, load_sem.at[3]),
        pltpu.make_async_copy(taps_hbm, taps_recv.at[s], load_sem.at[4]),
    ]
    for load in loads:
        load.start()

    barrier = pltpu.get_barrier_semaphore()
    greeted = [((s + i) % SEQ, c) for i in range(1, SEQ) for c in sharing]
    greeted += [(s, c) for c in sharing[1:]]
    greeted += [(s, chan(yh, z + i, core)) for i in (1, -1, 2, -2)]
    for target in greeted:
        pl.semaphore_signal(barrier, inc=1, device_id=target, device_id_type=MESH)

    def remote(src, dst, send, recv, target):
        pltpu.make_async_remote_copy(
            src_ref=src, dst_ref=dst, send_sem=send, recv_sem=recv,
            device_id=target, device_id_type=MESH,
        ).start()

    w_rows = pl.ds(aligned((yh * 2 + core) * WIDTH, WIDTH), WIDTH)

    def w_block(place, y, c):
        block = chan(y, z + PLACES[place], c)
        return w_hbm.at[:, pl.ds(aligned(block * WIDTH, WIDTH), WIDTH)]

    def w_slot(place):
        return wbuf.at[w_rows, pl.ds(place * WIDTH, WIDTH)]

    for place in range(RING):
        pltpu.make_async_copy(w_block(place, yh, core), w_slot(place), w_near.at[place // 2]).start()

    loads[0].wait()
    loads[1].wait()
    mixed = (k_in[...].astype(F32) * v_in[...].astype(F32)).astype(BF)
    m_send[...] = mixed.astype(F32).T.astype(BF)
    loads[2].wait()
    q_send[...] = q_in[...].astype(F32).T.astype(BF)
    mine = pl.ds(aligned(s * GROUP, GROUP), GROUP)
    m_recv[mine, :] = m_send[mine, :]
    q_recv[mine, :] = q_send[mine, :]
    loads[3].wait()
    loads[4].wait()

    pl.semaphore_wait(barrier, len(greeted))

    peers = [(s + i) % SEQ for i in range(1, SEQ)]
    for p in peers:
        remote(taps_hbm, taps_recv.at[s], send_sem.at[0], a2a_sem.at[0], (p, k))
    for p in peers:
        rows = pl.ds(aligned(p * GROUP, GROUP), GROUP)
        remote(m_send.at[rows, :], m_recv.at[mine, :], send_sem.at[1], a2a_sem.at[1], (p, k))
    for p in peers:
        rows = pl.ds(aligned(p * GROUP, GROUP), GROUP)
        remote(q_send.at[rows, :], q_recv.at[mine, :], send_sem.at[2], a2a_sem.at[2], (p, k))

    def send_far(pair):
        for place in (2 * pair, 2 * pair + 1):
            for seq, target, c in far_rows:
                remote(
                    w_block(place, 1 - yh, c), w_slot(place), send_sem.at[3], w_far.at[pair],
                    (seq, target),
                )

    for place in range(RING):
        remote(
            w_block(place, yh, 1 - core), w_slot(place), send_sem.at[3], w_far.at[place // 2],
            (s, mate),
        )
    for pair in range(FIRST_PAIRS):
        send_far(pair)

    wait_bytes(taps_recv.at[pl.ds(0, SEQ - 1)], a2a_sem.at[0])
    all_taps = taps_recv[...].astype(F32)
    group_row = lax.broadcasted_iota(jnp.int32, all_taps.shape, 1)
    taps = jnp.sum(jnp.where(group_row == s, all_taps, 0.0), axis=1)
    row = lax.broadcasted_iota(jnp.int32, (ROWS, ROWS), 0)
    col = lax.broadcasted_iota(jnp.int32, (ROWS, ROWS), 1)
    upper = col >= row
    before = jnp.zeros((ROWS, ROWS), F32)
    for d in range(SEQ):
        spread = jnp.broadcast_to(taps[d : d + 1, :], (ROWS, ROWS))
        rolled = pltpu.roll(spread, 0, 1, stride=1, stride_axis=0)
        tmat[d] = jnp.where(upper, rolled, before).astype(BF)
        before = rolled

    lane = lax.broadcasted_iota(jnp.int32, (WIDTH, WIDTH), 1)
    line = lax.broadcasted_iota(jnp.int32, (WIDTH, WIDTH), 0)
    picked = jnp.where(lane == s * GROUP + line % GROUP, jnp.broadcast_to(gain[...], (WIDTH, WIDTH)), 0.0)
    row_gain = jnp.sum(picked, axis=1, keepdims=True)

    wait_bytes(m_recv.at[pl.ds(0, GROUP * (SEQ - 1)), :], a2a_sem.at[1])
    conv[...] = jnp.dot(m_recv[...], tmat[0], preferred_element_type=F32)
    for d in range(1, SEQ):
        kept = WIDTH - GROUP * d
        conv[GROUP * d :, :] += jnp.dot(m_recv[:kept, :], tmat[d], preferred_element_type=F32)
    wait_bytes(q_recv.at[pl.ds(0, GROUP * (SEQ - 1)), :], a2a_sem.at[2])
    gated = q_recv[...].astype(F32) * (conv[...] + row_gain * m_recv[...].astype(F32))
    for h in range(2):
        g_send[h] = gated[:, h * HALF : (h + 1) * HALF].astype(BF)

    land = pl.ds(aligned((yh * 2 + core) * WIDTH + s * GROUP, GROUP), GROUP)
    for h in range(2):
        for p in peers:
            rows = pl.ds(aligned(p * GROUP, GROUP), GROUP)
            for c in sharing:
                remote(g_send.at[h, rows, :], g_recv.at[h, land, :], send_sem.at[4], g_sem.at[h], (p, c))
        for c in sharing[1:]:
            remote(g_send.at[h, mine, :], g_recv.at[h, land, :], send_sem.at[4], g_sem.at[h], (s, c))
        g_recv[h, land, :] = g_send[h, mine, :]
    for pair in range(FIRST_PAIRS, PAIRS):
        send_far(pair)

    def wait_w(pair):
        wait_bytes(wbuf.at[pl.ds(0, WIDTH), pl.ds(0, 2 * WIDTH)], w_near.at[pair])
        wait_bytes(wbuf.at[pl.ds(0, 3 * WIDTH), pl.ds(0, 2 * WIDTH)], w_far.at[pair])

    def product(rows, pair):
        return jnp.dot(
            rows, wbuf[:, 2 * pair * WIDTH : 2 * (pair + 1) * WIDTH], preferred_element_type=F32
        )

    def give(kind, h, value, distance):
        out_send[kind, h] = value.astype(BF)
        remote(
            out_send.at[kind, h], out_recv.at[kind, h], send_sem.at[5], out_sem.at[2 * kind + h],
            (s, chan(yh, z + distance, core)),
        )

    def take(kind, h):
        wait_bytes(out_recv.at[kind, h], out_sem.at[2 * kind + h])
        return out_recv[kind, h].astype(F32)

    for h in range(2):
        wait_bytes(g_recv.at[h, pl.ds(0, 4 * WIDTH - GROUP), :], g_sem.at[h])
        g_rows[h] = g_recv[h].astype(F32).T.astype(BF)
        if h == 0:
            wait_w(0)
        both = product(g_rows[h], 0)
        give(R4, h, both[:, :WIDTH], 2 if h == 0 else -2)
        give(UP3, h, both[:, WIDTH:], 1)
        if h == 0:
            wait_w(1)
        both = product(g_rows[h], 1)
        give(DOWN3, h, both[:, :WIDTH], -1)
        give(UP1, h, both[:, WIDTH:], 1)
    wait_w(2)
    for h in range(2):
        both = product(g_rows[h], 2)
        give(DOWN1, h, both[:, :WIDTH], -1)
        part[0, h] = both[:, WIDTH:]
    wait_w(3)
    for h in range(2):
        both = product(g_rows[h], 3)
        part[1, h] = both[:, :WIDTH]
        part[2, h] = both[:, WIDTH:]

    give(DOWN2, 0, part[1, 0] + take(DOWN3, 0), -2)
    give(UP2, 0, part[0, 0] + take(UP3, 0) + take(R4, 0), 2)
    give(UP2, 1, part[0, 1] + take(UP3, 1), 2)
    give(DOWN2, 1, part[1, 1] + take(DOWN3, 1) + take(R4, 1), -2)
    for h in range(2):
        total = part[2, h] + take(UP1, h) + take(DOWN1, h)
        part[2, h] = total
    for h in range(2):
        total = part[2, h] + take(UP2, h) + take(DOWN2, h)
        out_ref[pl.ds(h * HALF, HALF), :] = total.astype(BF)

    wait_bytes(taps_recv.at[pl.ds(0, SEQ - 1)], send_sem.at[0])
    wait_bytes(m_recv.at[pl.ds(0, GROUP * (SEQ - 1)), :], send_sem.at[1])
    wait_bytes(q_recv.at[pl.ds(0, GROUP * (SEQ - 1)), :], send_sem.at[2])
    wait_bytes(wbuf.at[pl.ds(0, 3 * WIDTH), :], send_sem.at[3])
    wait_bytes(g_recv.at[0, pl.ds(0, 4 * WIDTH - GROUP), :], send_sem.at[4])
    wait_bytes(g_recv.at[1, pl.ds(0, 4 * WIDTH - GROUP), :], send_sem.at[4])
    wait_bytes(out_send, send_sem.at[5])


def body(query_in, key_in, value_in, filter_taps, skip_gain, out_weight):
    dma = pltpu.SemaphoreType.DMA
    hbm = pl.BlockSpec(memory_space=pltpu.MemorySpace.HBM)
    return pl.pallas_call(
        kernel,
        out_shape=jax.ShapeDtypeStruct((ROWS, WIDTH), BF),
        in_specs=[hbm] * 6,
        out_specs=pl.BlockSpec(memory_space=pltpu.VMEM),
        scratch_shapes=[
            pltpu.VMEM((ROWS, WIDTH), BF),
            pltpu.VMEM((ROWS, WIDTH), BF),
            pltpu.VMEM((ROWS, WIDTH), BF),
            pltpu.VMEM((1, WIDTH), F32),
            pltpu.VMEM((4 * WIDTH, RING * WIDTH), BF),
            pltpu.VMEM((WIDTH, ROWS), BF),
            pltpu.VMEM((WIDTH, ROWS), BF),
            pltpu.VMEM((WIDTH, ROWS), BF),
            pltpu.VMEM((WIDTH, ROWS), BF),
            pltpu.VMEM((SEQ, SEQ, ROWS), BF),
            pltpu.VMEM((SEQ, ROWS, ROWS), BF),
            pltpu.VMEM((WIDTH, ROWS), F32),
            pltpu.VMEM((2, WIDTH, HALF), BF),
            pltpu.VMEM((2, 4 * WIDTH, HALF), BF),
            pltpu.VMEM((2, HALF, 4 * WIDTH), BF),
            pltpu.VMEM((3, 2, HALF, WIDTH), F32),
            pltpu.VMEM((7, 2, HALF, WIDTH), BF),
            pltpu.VMEM((7, 2, HALF, WIDTH), BF),
            dma((5,)),
            dma((PAIRS,)),
            dma((PAIRS,)),
            dma((3,)),
            dma((2,)),
            dma((14,)),
            dma((6,)),
        ],
        compiler_params=pltpu.CompilerParams(collective_id=0, has_side_effects=True),
    )(query_in, key_in, value_in, filter_taps, skip_gain.reshape(1, WIDTH), out_weight)


def solution(mesh):
    placed = (
        P("seq", "chan"),
        P("seq", "chan"),
        P("seq", "chan"),
        P("chan", "seq"),
        P("chan"),
        P("chan", None),
    )
    return jax.shard_map(
        body, mesh=mesh, in_specs=placed, out_specs=P("seq", "chan"), check_vma=False
    )
```

time: 38.1 us -> 35.4 us (0.929)
  the two profiles are of different devices: /device:TPU:64 before, /device:TPU:1 now
where the time goes in v2:
time: 35.4 us; the launch traced here: 35.2 us
  Pallas kernels  33.7 us (95%)
  local copies, waits for them, and re-layouts  1.47 us (4%)
    pallas_call x1, Pallas kernels, body(): pl.pallas_call(kernel, out_shape=jax.ShapeDtypeStruct((ROWS, WIDTH), BF),...  33.7 us
    unnamed x1, local copies, waits for them, and re-layouts  1.47 us

profile of v2, /device:TPU:1, one launch (start us, length us, event | category | flops | bytes accessed | tf_op | source)
XLA Modules:
  0.0 35.2 jit_solution(17058008744764039847)
XLA Ops:
  0.0 33.7 %shard_map.64 = bf16[256,128]{1,0:T(8,128)(2,1)} custom-call(bf16[256,128]{1,0:T(8,128)(2,1)} %q_hbm.1, bf16[256,128]{1,0:T(8,128)(2,1)} %k_hbm.1, bf16[256,128]{1,0:T(8,128)(2,1)} %v_hbm.1, bf16[8,256]{1,0:T(8,128)(2,1)} %taps_hbm.1, f32[1,128]{1,0:T(1,128)} %bitcast.1, bf16[128,4096]{1,0:T(8,128)(2,1)} %w_hbm.1), custom_call_target="tpu_custom_call" | custom-call | tf_op jit(solution)/shard_map/pallas_call | solution.py:237
  33.7 1.5 %copy.8 = bf16[256,128]{1,0:T(8,128)(2,1)} copy(bf16[256,128]{1,0:T(8,128)(2,1)} %shard_map.64) | data formatting | bytes 131072

commit v3 on v2

v3 whole, which is shorter than its diff:
```python
import functools

import jax
import jax.numpy as jnp
from jax import lax
from jax.experimental import pallas as pl
from jax.experimental.pallas import tpu as pltpu
from jax.sharding import PartitionSpec as P

MESH = pl.DeviceIdType.MESH
BF = jnp.bfloat16
F32 = jnp.float32
SEQ = 8
RING = 8
ROWS = 256
WIDTH = 128
GROUP = 16
HALF = 128
DEEP = ((4, 3), (5,), (7, 1))
SHALLOW = (2, 6, 0)
FIRST = 2
SUB = 1
PIECE = HALF // SUB
DELTAS = ((1, 2), (0, 2), (1, 1), (1, 3), (1, 0), (0, 1), (0, 3))
R4, UP3, DOWN3, UP1, DOWN1, UP2, DOWN2, OVER2, OVER6, OVER0 = range(10)


def aligned(value, multiple):
    return pl.multiple_of(value, multiple)


def wait_bytes(ref, sem):
    pltpu.make_async_copy(ref, ref, sem).wait()


def kernel(
    q_hbm, k_hbm, v_hbm, taps_hbm, gain_hbm, w_hbm, out_ref,
    q_in, k_in, v_in, gain, w_deep, w_flat,
    m_send, q_send, m_recv, q_recv, taps_recv, tmat, conv, g_send, g_recv, g_rows,
    part, out_send, out_recv,
    load_sem, w_near, w_far, a2a_sem, g_sem, out_sem, send_sem,
):
    s = lax.axis_index("seq")
    k = lax.axis_index("chan")
    core = k % 2
    z = (k // 2) % RING
    yh = k // (2 * RING)

    def chan(y, level, c):
        return y * (2 * RING) + ((level + RING) % RING) * 2 + c

    mate = chan(yh, z, 1 - core)
    sharing = [(chan(y, z, c), yr) for yr, y in ((1, 1 - yh), (0, yh)) for c in (1 - core, core)]
    x, ylo = s % 4, s // 4
    near = ((ylo + 1) % 2) * 4 + x
    peers = [((ylo + dy) % 2) * 4 + (x + dx) % 4 for dy, dx in DELTAS]
    far_rows = [(near, chan(1 - yh, z, c), c) for c in (core, 1 - core)]

    loads = [
        pltpu.make_async_copy(k_hbm, k_in, load_sem.at[0]),
        pltpu.make_async_copy(v_hbm, v_in, load_sem.at[1]),
        pltpu.make_async_copy(q_hbm, q_in, load_sem.at[2]),
        pltpu.make_async_copy(gain_hbm, gain, load_sem.at[3]),
        pltpu.make_async_copy(taps_hbm, taps_recv.at[s], load_sem.at[4]),
    ]
    for load in loads:
        load.start()

    barrier = pltpu.get_barrier_semaphore()
    greeted = [(p, c) for p in peers for c, _ in sharing]
    greeted += [(s, c) for c, _ in sharing[:3]]
    greeted += [(s, chan(yh, z + i, core)) for i in (1, -1, 2, -2)]
    for target in greeted:
        pl.semaphore_signal(barrier, inc=1, device_id=target, device_id_type=MESH)

    def remote(src, dst, send, recv, target):
        pltpu.make_async_remote_copy(
            src_ref=src, dst_ref=dst, send_sem=send, recv_sem=recv,
            device_id=target, device_id_type=MESH,
        ).start()


    def w_block(y, distance, c):
        block = chan(y, z + distance, c)
        return w_hbm.at[:, pl.ds(aligned(block * WIDTH, WIDTH), WIDTH)]

    def w_rows(yr):
        return pl.ds(aligned(yr * 2 * WIDTH + core * WIDTH, WIDTH), WIDTH)

    slots = {r: n for n, r in enumerate(r for group in DEEP for r in group)}

    def deep_slot(r, yr):
        return w_deep.at[w_rows(yr), pl.ds(slots[r] * WIDTH, WIDTH)]

    def flat_slot(n):
        return w_flat.at[w_rows(0), pl.ds(n * WIDTH, WIDTH)]

    flat_blocks = [(yh, r) for r in SHALLOW[:2]] + [(1 - yh, r) for r in SHALLOW[:2]]
    flat_blocks += [(yh, SHALLOW[2]), (1 - yh, SHALLOW[2])]

    for n, group in enumerate(DEEP):
        for r in group:
            pltpu.make_async_copy(w_block(yh, r, core), deep_slot(r, 0), w_near.at[n]).start()
    for n, (y, r) in enumerate(flat_blocks):
        pltpu.make_async_copy(w_block(y, r, core), flat_slot(n), w_near.at[3]).start()

    loads[0].wait()
    loads[1].wait()
    mixed = (k_in[...].astype(F32) * v_in[...].astype(F32)).astype(BF)
    m_send[...] = mixed.astype(F32).T.astype(BF)
    loads[2].wait()
    q_send[...] = q_in[...].astype(F32).T.astype(BF)
    mine = pl.ds(aligned(s * GROUP, GROUP), GROUP)
    m_recv[mine, :] = m_send[mine, :]
    q_recv[mine, :] = q_send[mine, :]
    loads[3].wait()
    loads[4].wait()

    pl.semaphore_wait(barrier, len(greeted))

    for p in peers:
        remote(taps_hbm, taps_recv.at[s], send_sem.at[0], a2a_sem.at[0], (p, k))
    for p in peers:
        rows = pl.ds(aligned(p * GROUP, GROUP), GROUP)
        remote(m_send.at[rows, :], m_recv.at[mine, :], send_sem.at[1], a2a_sem.at[1], (p, k))
    for p in peers:
        rows = pl.ds(aligned(p * GROUP, GROUP), GROUP)
        remote(q_send.at[rows, :], q_recv.at[mine, :], send_sem.at[2], a2a_sem.at[2], (p, k))

    def send_far(n):
        for r in DEEP[n]:
            for seq, target, c in far_rows:
                remote(w_block(1 - yh, r, c), deep_slot(r, 1), send_sem.at[3], w_far.at[n], (seq, target))

    for n in range(FIRST):
        send_far(n)
    for n, group in enumerate(DEEP):
        for r in group:
            remote(w_block(yh, r, 1 - core), deep_slot(r, 0), send_sem.at[3], w_far.at[n], (s, mate))
    for n, (y, r) in enumerate(flat_blocks):
        remote(w_block(y, r, 1 - core), flat_slot(n), send_sem.at[3], w_far.at[3], (s, mate))

    wait_bytes(taps_recv.at[pl.ds(0, SEQ - 1)], a2a_sem.at[0])
    all_taps = taps_recv[...].astype(F32)
    group_row = lax.broadcasted_iota(jnp.int32, all_taps.shape, 1)
    taps = jnp.sum(jnp.where(group_row == s, all_taps, 0.0), axis=1)
    row = lax.broadcasted_iota(jnp.int32, (ROWS, ROWS), 0)
    col = lax.broadcasted_iota(jnp.int32, (ROWS, ROWS), 1)
    upper = col >= row
    before = jnp.zeros((ROWS, ROWS), F32)
    for d in range(SEQ):
        spread = jnp.broadcast_to(taps[d : d + 1, :], (ROWS, ROWS))
        rolled = pltpu.roll(spread, 0, 1, stride=1, stride_axis=0)
        tmat[d] = jnp.where(upper, rolled, before).astype(BF)
        before = rolled

    lane = lax.broadcasted_iota(jnp.int32, (WIDTH, WIDTH), 1)
    line = lax.broadcasted_iota(jnp.int32, (WIDTH, WIDTH), 0)
    picked = jnp.where(lane == s * GROUP + line % GROUP, jnp.broadcast_to(gain[...], (WIDTH, WIDTH)), 0.0)
    row_gain = jnp.sum(picked, axis=1, keepdims=True)

    wait_bytes(m_recv.at[pl.ds(0, GROUP * (SEQ - 1)), :], a2a_sem.at[1])
    conv[...] = jnp.dot(m_recv[...], tmat[0], preferred_element_type=F32)
    for d in range(1, SEQ):
        kept = WIDTH - GROUP * d
        conv[GROUP * d :, :] += jnp.dot(m_recv[:kept, :], tmat[d], preferred_element_type=F32)
    wait_bytes(q_recv.at[pl.ds(0, GROUP * (SEQ - 1)), :], a2a_sem.at[2])
    gated = q_recv[...].astype(F32) * (conv[...] + row_gain * m_recv[...].astype(F32))
    for h in range(2):
        g_send[h] = gated[:, h * HALF : (h + 1) * HALF].astype(BF)

    def land(yr):
        return pl.ds(aligned(yr * 2 * WIDTH + core * WIDTH + s * GROUP, GROUP), GROUP)

    for h in range(2):
        for p in (*peers[:5], None, *peers[5:]):
            rows = mine if p is None else pl.ds(aligned(p * GROUP, GROUP), GROUP)
            for c, yr in sharing if p is not None else sharing[:3]:
                remote(
                    g_send.at[h, rows, :], g_recv.at[h, land(yr), :], send_sem.at[4], g_sem.at[h],
                    (s if p is None else p, c),
                )
        g_recv[h, land(0), :] = g_send[h, mine, :]
    for n in range(FIRST, len(DEEP)):
        send_far(n)

    def wait_deep(n):
        columns = pl.ds(0, len(DEEP[n]) * WIDTH)
        wait_bytes(w_deep.at[pl.ds(0, WIDTH), columns], w_near.at[n])
        wait_bytes(w_deep.at[pl.ds(0, 3 * WIDTH), columns], w_far.at[n])

    def deep(h, n):
        first = slots[DEEP[n][0]] * WIDTH
        return jnp.dot(
            g_rows[h], w_deep[:, first : first + len(DEEP[n]) * WIDTH], preferred_element_type=F32
        )

    def flat(h, n):
        return jnp.dot(
            g_rows[h, :, : 2 * WIDTH], w_flat[:, n * 2 * WIDTH : (n + 1) * 2 * WIDTH],
            preferred_element_type=F32,
        )

    def give(kind, h, c, value, distance):
        piece = pl.ds(c * PIECE, PIECE)
        out_send[kind, h, piece, :] = value.astype(BF)
        target = chan(1 - yh, z, core) if kind >= OVER2 else chan(yh, z + distance, core)
        remote(
            out_send.at[kind, h, piece, :], out_recv.at[kind, h, piece, :],
            send_sem.at[5], out_sem.at[(2 * kind + h) * SUB + c], (s, target),
        )

    def take(kind, h, c):
        piece = pl.ds(c * PIECE, PIECE)
        wait_bytes(out_recv.at[kind, h, piece, :], out_sem.at[(2 * kind + h) * SUB + c])
        return out_recv[kind, h, piece, :].astype(F32)

    def cut(value, c):
        return value[c * PIECE : (c + 1) * PIECE]

    for h in range(2):
        wait_bytes(g_recv.at[h, pl.ds(0, 4 * WIDTH - GROUP), :], g_sem.at[h])
        g_rows[h] = g_recv[h].astype(F32).T.astype(BF)
        if h == 0:
            wait_deep(0)
        both = deep(h, 0)
        for c in range(SUB):
            give(R4, h, c, cut(both[:, :WIDTH], c), 2 if h == 0 else -2)
            give(UP3, h, c, cut(both[:, WIDTH:], c), 1)
        if h == 0:
            wait_deep(1)
        one = deep(h, 1)
        for c in range(SUB):
            give(DOWN3, h, c, cut(one, c), -1)
        if h == 0:
            wait_bytes(w_flat.at[pl.ds(0, WIDTH), :], w_near.at[3])
            wait_bytes(w_flat.at[pl.ds(0, WIDTH), :], w_far.at[3])
        both = flat(h, 1)
        for c in range(SUB):
            give(OVER6, h, c, cut(both[:, WIDTH:], c), 0)
        for c in range(SUB):
            give(OVER2, h, c, cut(both[:, :WIDTH], c), 0)
    for h in range(2):
        both = flat(h, 0)
        part[0, h] = both[:, :WIDTH]
        part[1, h] = both[:, WIDTH:]
    wait_deep(2)
    for h in range(2):
        both = deep(h, 2)
        for c in range(SUB):
            give(DOWN1, h, c, cut(both[:, :WIDTH], c), -1)
        for c in range(SUB):
            give(UP1, h, c, cut(both[:, WIDTH:], c), 1)
    for h in range(2):
        both = flat(h, 2)
        part[2, h] = both[:, :WIDTH]
        for c in range(SUB):
            give(OVER0, h, c, cut(both[:, WIDTH:], c), 0)

    def second(kind, h):
        for c in range(SUB):
            piece = pl.ds(c * PIECE, PIECE)
            if kind == UP2:
                total = part[0, h, piece, :] + take(UP3, h, c) + take(OVER2, h, c)
            else:
                total = part[1, h, piece, :] + take(DOWN3, h, c) + take(OVER6, h, c)
            if (kind == UP2) == (h == 0):
                total = total + take(R4, h, c)
            give(kind, h, c, total, 2 if kind == UP2 else -2)

    second(DOWN2, 0)
    second(UP2, 0)
    second(UP2, 1)
    second(DOWN2, 1)
    for h in range(2):
        for c in range(SUB):
            piece = pl.ds(c * PIECE, PIECE)
            part[2, h, piece, :] = (
                part[2, h, piece, :] + take(UP1, h, c) + take(DOWN1, h, c) + take(OVER0, h, c)
            )
    for h in range(2):
        for c in range(SUB):
            piece = pl.ds(c * PIECE, PIECE)
            total = part[2, h, piece, :] + take(UP2, h, c) + take(DOWN2, h, c)
            out_ref[pl.ds(h * HALF + c * PIECE, PIECE), :] = total.astype(BF)

    wait_bytes(taps_recv.at[pl.ds(0, SEQ - 1)], send_sem.at[0])
    wait_bytes(m_recv.at[pl.ds(0, GROUP * (SEQ - 1)), :], send_sem.at[1])
    wait_bytes(q_recv.at[pl.ds(0, GROUP * (SEQ - 1)), :], send_sem.at[2])
    wait_bytes(w_deep.at[pl.ds(0, 3 * WIDTH), :], send_sem.at[3])
    wait_bytes(w_flat.at[pl.ds(0, WIDTH), :], send_sem.at[3])
    wait_bytes(g_recv.at[0, pl.ds(0, 4 * WIDTH - GROUP), :], send_sem.at[4])
    wait_bytes(g_recv.at[1, pl.ds(0, 4 * WIDTH - GROUP), :], send_sem.at[4])
    wait_bytes(out_send, send_sem.at[5])


def body(query_in, key_in, value_in, filter_taps, skip_gain, out_weight):
    dma = pltpu.SemaphoreType.DMA
    hbm = pl.BlockSpec(memory_space=pltpu.MemorySpace.HBM)
    skip_gain = skip_gain.reshape(1, WIDTH)
    operands = (query_in, key_in, value_in, filter_taps, skip_gain, out_weight)
    operands = [pltpu.with_memory_space_constraint(x, pltpu.MemorySpace.HBM) for x in operands]
    return pl.pallas_call(
        kernel,
        out_shape=jax.ShapeDtypeStruct((ROWS, WIDTH), BF),
        in_specs=[hbm] * 6,
        out_specs=pl.BlockSpec(memory_space=pltpu.VMEM),
        scratch_shapes=[
            pltpu.VMEM((ROWS, WIDTH), BF),
            pltpu.VMEM((ROWS, WIDTH), BF),
            pltpu.VMEM((ROWS, WIDTH), BF),
            pltpu.VMEM((1, WIDTH), F32),
            pltpu.VMEM((4 * WIDTH, 5 * WIDTH), BF),
            pltpu.VMEM((2 * WIDTH, 6 * WIDTH), BF),
            pltpu.VMEM((WIDTH, ROWS), BF),
            pltpu.VMEM((WIDTH, ROWS), BF),
            pltpu.VMEM((WIDTH, ROWS), BF),
            pltpu.VMEM((WIDTH, ROWS), BF),
            pltpu.VMEM((SEQ, SEQ, ROWS), BF),
            pltpu.VMEM((SEQ, ROWS, ROWS), BF),
            pltpu.VMEM((WIDTH, ROWS), F32),
            pltpu.VMEM((2, WIDTH, HALF), BF),
            pltpu.VMEM((2, 4 * WIDTH, HALF), BF),
            pltpu.VMEM((2, HALF, 4 * WIDTH), BF),
            pltpu.VMEM((3, 2, HALF, WIDTH), F32),
            pltpu.VMEM((10, 2, HALF, WIDTH), BF),
            pltpu.VMEM((10, 2, HALF, WIDTH), BF),
            dma((5,)),
            dma((4,)),
            dma((4,)),
            dma((3,)),
            dma((2,)),
            dma((20 * SUB,)),
            dma((6,)),
        ],
        compiler_params=pltpu.CompilerParams(collective_id=0, has_side_effects=True, vmem_limit_bytes=24 * 1024 * 1024),
    )(*operands)


def solution(mesh):
    placed = (
        P("seq", "chan"),
        P("seq", "chan"),
        P("seq", "chan"),
        P("chan", "seq"),
        P("chan"),
        P("chan", None),
    )
    return jax.shard_map(
        body, mesh=mesh, in_specs=placed, out_specs=P("seq", "chan"), check_vma=False
    )
```

time: 35.4 us -> 32.3 us (0.912)
  the two profiles are of different devices: /device:TPU:1 before, /device:TPU:30 now
where the time goes in v3:
time: 32.3 us; the launch traced here: 32.2 us
  Pallas kernels  31.6 us (98%)
  local copies, waits for them, and re-layouts  0.63 us (2%)
    pallas_call x1, Pallas kernels, body(): pl.pallas_call(kernel, out_shape=jax.ShapeDtypeStruct((ROWS, WIDTH), BF),...  31.6 us

profile of v3, /device:TPU:30, one launch (start us, length us, event | category | flops | bytes accessed | tf_op | source)
XLA Modules:
  0.0 32.2 jit_solution(13354084116338866157)
XLA Ops:
  0.0 31.6 %shard_map.64 = bf16[256,128]{1,0:T(8,128)(2,1)S(1)} custom-call(bf16[256,128]{1,0:T(8,128)(2,1)} %q_hbm.1, bf16[256,128]{1,0:T(8,128)(2,1)} %k_hbm.1, bf16[256,128]{1,0:T(8,128)(2,1)} %v_hbm.1, bf16[8,256]{1,0:T(8,128)(2,1)} %taps_hbm.1, f32[1,128]{1,0:T(1,128)} %bitcast.1, bf16[128,4096]{1,0:T(8,128)(2,1)} %w_hbm.1), custom_call_target="tpu_custom_call" | custom-call | tf_op jit(solution)/shard_map/pallas_call | solution.py:303
  31.6 0.6 %copy.8 = bf16[256,128]{1,0:T(8,128)(2,1)} copy(bf16[256,128]{1,0:T(8,128)(2,1)S(1)} %shard_map.64) | data formatting | bytes 131072

commit v4 on v3

--- a/solution.py
+++ b/solution.py
@@ -36,9 +36,9 @@
 def kernel(
     q_hbm, k_hbm, v_hbm, taps_hbm, gain_hbm, w_hbm, out_ref,
     q_in, k_in, v_in, gain, w_deep, w_flat,
-    m_send, q_send, m_recv, q_recv, taps_recv, tmat, conv, g_send, g_recv, g_rows,
+    m_send, q_send, m_recv, q_recv, taps_in, taps_send, taps_recv, tmat, conv, g_send, g_recv, g_rows,
     part, out_send, out_recv,
-    load_sem, w_near, w_far, a2a_sem, g_sem, out_sem, send_sem,
+    load_sem, w_near, w_far, a2a_sem, g_sem, relay_sem, out_sem, send_sem,
 ):
     s = lax.axis_index("seq")
     k = lax.axis_index("chan")
@@ -61,14 +61,15 @@
         pltpu.make_async_copy(v_hbm, v_in, load_sem.at[1]),
         pltpu.make_async_copy(q_hbm, q_in, load_sem.at[2]),
         pltpu.make_async_copy(gain_hbm, gain, load_sem.at[3]),
-        pltpu.make_async_copy(taps_hbm, taps_recv.at[s], load_sem.at[4]),
+        pltpu.make_async_copy(taps_hbm, taps_in, load_sem.at[4]),
     ]
     for load in loads:
         load.start()
 
     barrier = pltpu.get_barrier_semaphore()
-    greeted = [(p, c) for p in peers for c, _ in sharing]
-    greeted += [(s, c) for c, _ in sharing[:3]]
+    same_core = [(chan(1 - yh, z, core), 1), (k, 0)]
+    greeted = [(p, c) for p in peers for c, _ in same_core]
+    greeted += [far_rows[1][:2], (s, same_core[0][0]), (s, mate)]
     greeted += [(s, chan(yh, z + i, core)) for i in (1, -1, 2, -2)]
     for target in greeted:
         pl.semaphore_signal(barrier, inc=1, device_id=target, device_id_type=MESH)
@@ -115,11 +116,14 @@
     q_recv[mine, :] = q_send[mine, :]
     loads[3].wait()
     loads[4].wait()
+    for n in range(SEQ):
+        taps_send[n] = taps_in[n : n + 1, :].astype(F32)
+    taps_recv[s] = taps_send[s]
 
     pl.semaphore_wait(barrier, len(greeted))
 
     for p in peers:
-        remote(taps_hbm, taps_recv.at[s], send_sem.at[0], a2a_sem.at[0], (p, k))
+        remote(taps_send.at[p], taps_recv.at[s], send_sem.at[0], a2a_sem.at[0], (p, k))
     for p in peers:
         rows = pl.ds(aligned(p * GROUP, GROUP), GROUP)
         remote(m_send.at[rows, :], m_recv.at[mine, :], send_sem.at[1], a2a_sem.at[1], (p, k))
@@ -141,15 +145,12 @@
         remote(w_block(y, r, 1 - core), flat_slot(n), send_sem.at[3], w_far.at[3], (s, mate))
 
     wait_bytes(taps_recv.at[pl.ds(0, SEQ - 1)], a2a_sem.at[0])
-    all_taps = taps_recv[...].astype(F32)
-    group_row = lax.broadcasted_iota(jnp.int32, all_taps.shape, 1)
-    taps = jnp.sum(jnp.where(group_row == s, all_taps, 0.0), axis=1)
     row = lax.broadcasted_iota(jnp.int32, (ROWS, ROWS), 0)
     col = lax.broadcasted_iota(jnp.int32, (ROWS, ROWS), 1)
     upper = col >= row
     before = jnp.zeros((ROWS, ROWS), F32)
     for d in range(SEQ):
-        spread = jnp.broadcast_to(taps[d : d + 1, :], (ROWS, ROWS))
+        spread = jnp.broadcast_to(taps_recv[d], (ROWS, ROWS))
         rolled = pltpu.roll(spread, 0, 1, stride=1, stride_axis=0)
         tmat[d] = jnp.where(upper, rolled, before).astype(BF)
         before = rolled
@@ -175,7 +176,7 @@
     for h in range(2):
         for p in (*peers[:5], None, *peers[5:]):
             rows = mine if p is None else pl.ds(aligned(p * GROUP, GROUP), GROUP)
-            for c, yr in sharing if p is not None else sharing[:3]:
+            for c, yr in same_core if p is not None else same_core[:1]:
                 remote(
                     g_send.at[h, rows, :], g_recv.at[h, land(yr), :], send_sem.at[4], g_sem.at[h],
                     (s if p is None else p, c),
@@ -218,28 +219,50 @@
     def cut(value, c):
         return value[c * PIECE : (c + 1) * PIECE]
 
-    for h in range(2):
-        wait_bytes(g_recv.at[h, pl.ds(0, 4 * WIDTH - GROUP), :], g_sem.at[h])
+    def relay(h):
+        wait_bytes(g_recv.at[h, pl.ds(0, 2 * WIDTH - GROUP), :], g_sem.at[h])
+        for yr in range(2):
+            remote(
+                g_recv.at[h, w_rows(yr), :], g_recv.at[h, w_rows(yr), :], send_sem.at[6],
+                relay_sem.at[h], (s, mate),
+            )
+
+    def turn(h):
+        wait_bytes(g_recv.at[h, pl.ds(0, 2 * WIDTH), :], relay_sem.at[h])
         g_rows[h] = g_recv[h].astype(F32).T.astype(BF)
-        if h == 0:
-            wait_deep(0)
+
+    def first(h):
         both = deep(h, 0)
         for c in range(SUB):
             give(R4, h, c, cut(both[:, :WIDTH], c), 2 if h == 0 else -2)
             give(UP3, h, c, cut(both[:, WIDTH:], c), 1)
-        if h == 0:
-            wait_deep(1)
+
+    def first_down(h):
         one = deep(h, 1)
         for c in range(SUB):
             give(DOWN3, h, c, cut(one, c), -1)
-        if h == 0:
-            wait_bytes(w_flat.at[pl.ds(0, WIDTH), :], w_near.at[3])
-            wait_bytes(w_flat.at[pl.ds(0, WIDTH), :], w_far.at[3])
+
+    def over(h):
         both = flat(h, 1)
         for c in range(SUB):
             give(OVER6, h, c, cut(both[:, WIDTH:], c), 0)
         for c in range(SUB):
             give(OVER2, h, c, cut(both[:, :WIDTH], c), 0)
+
+    relay(0)
+    wait_deep(0)
+    wait_deep(1)
+    turn(0)
+    first(0)
+    first_down(0)
+    relay(1)
+    wait_bytes(w_flat.at[pl.ds(0, WIDTH), :], w_near.at[3])
+    wait_bytes(w_flat.at[pl.ds(0, WIDTH), :], w_far.at[3])
+    over(0)
+    turn(1)
+    first(1)
+    first_down(1)
+    over(1)
     for h in range(2):
         both = flat(h, 0)
         part[0, h] = both[:, :WIDTH]
@@ -289,8 +312,8 @@
     wait_bytes(q_recv.at[pl.ds(0, GROUP * (SEQ - 1)), :], send_sem.at[2])
     wait_bytes(w_deep.at[pl.ds(0, 3 * WIDTH), :], send_sem.at[3])
     wait_bytes(w_flat.at[pl.ds(0, WIDTH), :], send_sem.at[3])
-    wait_bytes(g_recv.at[0, pl.ds(0, 4 * WIDTH - GROUP), :], send_sem.at[4])
-    wait_bytes(g_recv.at[1, pl.ds(0, 4 * WIDTH - GROUP), :], send_sem.at[4])
+    wait_bytes(g_recv.at[0, pl.ds(0, 4 * WIDTH - 2 * GROUP), :], send_sem.at[4])
+    wait_bytes(g_recv.at[0], send_sem.at[6])
     wait_bytes(out_send, send_sem.at[5])
 
 
@@ -316,7 +339,9 @@
             pltpu.VMEM((WIDTH, ROWS), BF),
             pltpu.VMEM((WIDTH, ROWS), BF),
             pltpu.VMEM((WIDTH, ROWS), BF),
-            pltpu.VMEM((SEQ, SEQ, ROWS), BF),
+            pltpu.VMEM((SEQ, ROWS), BF),
+            pltpu.VMEM((SEQ, 1, ROWS), F32),
+            pltpu.VMEM((SEQ, 1, ROWS), F32),
             pltpu.VMEM((SEQ, ROWS, ROWS), BF),
             pltpu.VMEM((WIDTH, ROWS), F32),
             pltpu.VMEM((2, WIDTH, HALF), BF),
@@ -330,8 +355,9 @@
             dma((4,)),
             dma((3,)),
             dma((2,)),
+            dma((2,)),
             dma((20 * SUB,)),
-            dma((6,)),
+            dma((7,)),
         ],
         compiler_params=pltpu.CompilerParams(collective_id=0, has_side_effects=True, vmem_limit_bytes=24 * 1024 * 1024),
     )(*operands)

time: 32.3 us -> 31.1 us (0.963)
  the two profiles are of different devices: /device:TPU:30 before, /device:TPU:1 now
where the time goes in v4:
time: 31.1 us; the launch traced here: 30.6 us
  Pallas kernels  30 us (96%)
  local copies, waits for them, and re-layouts  0.63 us (2%)
    pallas_call x1, Pallas kernels, body(): pl.pallas_call(kernel, out_shape=jax.ShapeDtypeStruct((ROWS, WIDTH), BF),...  30 us
    unnamed x1, local copies, waits for them, and re-layouts  0.63 us

profile of v4, /device:TPU:1, one launch (start us, length us, event | category | flops | bytes accessed | tf_op | source)
XLA Modules:
  0.0 30.6 jit_solution(2629953822571995788)
XLA Ops:
  0.0 30.0 %shard_map.64 = bf16[256,128]{1,0:T(8,128)(2,1)S(1)} custom-call(bf16[256,128]{1,0:T(8,128)(2,1)} %q_hbm.1, bf16[256,128]{1,0:T(8,128)(2,1)} %k_hbm.1, bf16[256,128]{1,0:T(8,128)(2,1)} %v_hbm.1, bf16[8,256]{1,0:T(8,128)(2,1)} %taps_hbm.1, f32[1,128]{1,0:T(1,128)} %bitcast.1, bf16[128,4096]{1,0:T(8,128)(2,1)} %w_hbm.1), custom_call_target="tpu_custom_call" | custom-call | tf_op jit(solution)/shard_map/pallas_call | solution.py:326
  30.0 0.6 %copy.8 = bf16[256,128]{1,0:T(8,128)(2,1)} copy(bf16[256,128]{1,0:T(8,128)(2,1)S(1)} %shard_map.64) | data formatting | bytes 131072

commit v5 on v4

--- a/solution.py
+++ b/solution.py
@@ -20,6 +20,7 @@
 SHALLOW = (2, 6, 0)
 FIRST = 2
 SUB = 1
+RELAYED = 1
 PIECE = HALF // SUB
 DELTAS = ((1, 2), (0, 2), (1, 1), (1, 3), (1, 0), (0, 1), (0, 3))
 R4, UP3, DOWN3, UP1, DOWN1, UP2, DOWN2, OVER2, OVER6, OVER0 = range(10)
@@ -68,8 +69,8 @@
 
     barrier = pltpu.get_barrier_semaphore()
     same_core = [(chan(1 - yh, z, core), 1), (k, 0)]
-    greeted = [(p, c) for p in peers for c, _ in same_core]
-    greeted += [far_rows[1][:2], (s, same_core[0][0]), (s, mate)]
+    greeted = [(p, c) for p in peers for c, _ in sharing]
+    greeted += [(s, c) for c, _ in sharing[:3]]
     greeted += [(s, chan(yh, z + i, core)) for i in (1, -1, 2, -2)]
     for target in greeted:
         pl.semaphore_signal(barrier, inc=1, device_id=target, device_id_type=MESH)
@@ -174,9 +175,10 @@
         return pl.ds(aligned(yr * 2 * WIDTH + core * WIDTH + s * GROUP, GROUP), GROUP)
 
     for h in range(2):
+        targets = same_core if h == RELAYED else sharing
         for p in (*peers[:5], None, *peers[5:]):
             rows = mine if p is None else pl.ds(aligned(p * GROUP, GROUP), GROUP)
-            for c, yr in same_core if p is not None else same_core[:1]:
+            for c, yr in targets if p is not None else targets[:-1]:
                 remote(
                     g_send.at[h, rows, :], g_recv.at[h, land(yr), :], send_sem.at[4], g_sem.at[h],
                     (s if p is None else p, c),
@@ -220,15 +222,20 @@
         return value[c * PIECE : (c + 1) * PIECE]
 
     def relay(h):
+        if h != RELAYED:
+            return
         wait_bytes(g_recv.at[h, pl.ds(0, 2 * WIDTH - GROUP), :], g_sem.at[h])
         for yr in range(2):
             remote(
                 g_recv.at[h, w_rows(yr), :], g_recv.at[h, w_rows(yr), :], send_sem.at[6],
-                relay_sem.at[h], (s, mate),
+                relay_sem, (s, mate),
             )
 
     def turn(h):
-        wait_bytes(g_recv.at[h, pl.ds(0, 2 * WIDTH), :], relay_sem.at[h])
+        if h == RELAYED:
+            wait_bytes(g_recv.at[h, pl.ds(0, 2 * WIDTH), :], relay_sem)
+        else:
+            wait_bytes(g_recv.at[h, pl.ds(0, 4 * WIDTH - GROUP), :], g_sem.at[h])
         g_rows[h] = g_recv[h].astype(F32).T.astype(BF)
 
     def first(h):
@@ -312,8 +319,9 @@
     wait_bytes(q_recv.at[pl.ds(0, GROUP * (SEQ - 1)), :], send_sem.at[2])
     wait_bytes(w_deep.at[pl.ds(0, 3 * WIDTH), :], send_sem.at[3])
     wait_bytes(w_flat.at[pl.ds(0, WIDTH), :], send_sem.at[3])
-    wait_bytes(g_recv.at[0, pl.ds(0, 4 * WIDTH - 2 * GROUP), :], send_sem.at[4])
-    wait_bytes(g_recv.at[0], send_sem.at[6])
+    wait_bytes(g_recv.at[0, pl.ds(0, 2 * WIDTH - GROUP), :], send_sem.at[4])
+    wait_bytes(g_recv.at[0, pl.ds(0, 4 * WIDTH - GROUP), :], send_sem.at[4])
+    wait_bytes(g_recv.at[0, pl.ds(0, 2 * WIDTH), :], send_sem.at[6])
     wait_bytes(out_send, send_sem.at[5])
 
 
@@ -355,7 +363,7 @@
             dma((4,)),
             dma((3,)),
             dma((2,)),
-            dma((2,)),
+            dma,
             dma((20 * SUB,)),
             dma((7,)),
         ],

time: 31.1 us -> 30.6 us (0.984); the launches traced: 30.6 us -> 30.5 us
  no operation moved by 1% of the time
where the time goes in v5:
time: 30.6 us; the launch traced here: 30.5 us
  Pallas kernels  29.9 us (98%)
  local copies, waits for them, and re-layouts  0.63 us (2%)
    pallas_call x1, Pallas kernels, body(): pl.pallas_call(kernel, out_shape=jax.ShapeDtypeStruct((ROWS, WIDTH), BF),...  29.9 us
    unnamed x1, local copies, waits for them, and re-layouts  0.63 us

profile of v5, /device:TPU:1, one launch (start us, length us, event | category | flops | bytes accessed | tf_op | source)
XLA Modules:
  0.0 30.5 jit_solution(1436191100479881623)
XLA Ops:
  0.0 29.9 %shard_map.64 = bf16[256,128]{1,0:T(8,128)(2,1)S(1)} custom-call(bf16[256,128]{1,0:T(8,128)(2,1)} %q_hbm.1, bf16[256,128]{1,0:T(8,128)(2,1)} %k_hbm.1, bf16[256,128]{1,0:T(8,128)(2,1)} %v_hbm.1, bf16[8,256]{1,0:T(8,128)(2,1)} %taps_hbm.1, f32[1,128]{1,0:T(1,128)} %bitcast.1, bf16[128,4096]{1,0:T(8,128)(2,1)} %w_hbm.1), custom_call_target="tpu_custom_call" | custom-call | tf_op jit(solution)/shard_map/pallas_call | solution.py:334
  29.9 0.6 %copy.8 = bf16[256,128]{1,0:T(8,128)(2,1)} copy(bf16[256,128]{1,0:T(8,128)(2,1)S(1)} %shard_map.64) | data formatting | bytes 131072

commit v6 on v5

--- a/solution.py
+++ b/solution.py
@@ -100,21 +100,11 @@
     flat_blocks = [(yh, r) for r in SHALLOW[:2]] + [(1 - yh, r) for r in SHALLOW[:2]]
     flat_blocks += [(yh, SHALLOW[2]), (1 - yh, SHALLOW[2])]
 
-    for n, group in enumerate(DEEP):
-        for r in group:
-            pltpu.make_async_copy(w_block(yh, r, core), deep_slot(r, 0), w_near.at[n]).start()
-    for n, (y, r) in enumerate(flat_blocks):
-        pltpu.make_async_copy(w_block(y, r, core), flat_slot(n), w_near.at[3]).start()
-
     loads[0].wait()
     loads[1].wait()
     mixed = (k_in[...].astype(F32) * v_in[...].astype(F32)).astype(BF)
     m_send[...] = mixed.astype(F32).T.astype(BF)
-    loads[2].wait()
-    q_send[...] = q_in[...].astype(F32).T.astype(BF)
     mine = pl.ds(aligned(s * GROUP, GROUP), GROUP)
-    m_recv[mine, :] = m_send[mine, :]
-    q_recv[mine, :] = q_send[mine, :]
     loads[3].wait()
     loads[4].wait()
     for n in range(SEQ):
@@ -128,6 +118,8 @@
     for p in peers:
         rows = pl.ds(aligned(p * GROUP, GROUP), GROUP)
         remote(m_send.at[rows, :], m_recv.at[mine, :], send_sem.at[1], a2a_sem.at[1], (p, k))
+    loads[2].wait()
+    q_send[...] = q_in[...].astype(F32).T.astype(BF)
     for p in peers:
         rows = pl.ds(aligned(p * GROUP, GROUP), GROUP)
         remote(q_send.at[rows, :], q_recv.at[mine, :], send_sem.at[2], a2a_sem.at[2], (p, k))
@@ -144,6 +136,14 @@
             remote(w_block(yh, r, 1 - core), deep_slot(r, 0), send_sem.at[3], w_far.at[n], (s, mate))
     for n, (y, r) in enumerate(flat_blocks):
         remote(w_block(y, r, 1 - core), flat_slot(n), send_sem.at[3], w_far.at[3], (s, mate))
+
+    m_recv[mine, :] = m_send[mine, :]
+    q_recv[mine, :] = q_send[mine, :]
+    for n, group in enumerate(DEEP):
+        for r in group:
+            pltpu.make_async_copy(w_block(yh, r, core), deep_slot(r, 0), w_near.at[n]).start()
+    for n, (y, r) in enumerate(flat_blocks):
+        pltpu.make_async_copy(w_block(y, r, core), flat_slot(n), w_near.at[3]).start()
 
     wait_bytes(taps_recv.at[pl.ds(0, SEQ - 1)], a2a_sem.at[0])
     row = lax.broadcasted_iota(jnp.int32, (ROWS, ROWS), 0)
@@ -162,19 +162,25 @@
     row_gain = jnp.sum(picked, axis=1, keepdims=True)
 
     wait_bytes(m_recv.at[pl.ds(0, GROUP * (SEQ - 1)), :], a2a_sem.at[1])
-    conv[...] = jnp.dot(m_recv[...], tmat[0], preferred_element_type=F32)
-    for d in range(1, SEQ):
-        kept = WIDTH - GROUP * d
-        conv[GROUP * d :, :] += jnp.dot(m_recv[:kept, :], tmat[d], preferred_element_type=F32)
-    wait_bytes(q_recv.at[pl.ds(0, GROUP * (SEQ - 1)), :], a2a_sem.at[2])
-    gated = q_recv[...].astype(F32) * (conv[...] + row_gain * m_recv[...].astype(F32))
-    for h in range(2):
-        g_send[h] = gated[:, h * HALF : (h + 1) * HALF].astype(BF)
+    skip = row_gain * m_recv[...].astype(F32)
+
+    def gate(h):
+        side = slice(h * HALF, (h + 1) * HALF)
+        conv[:, side] = jnp.dot(m_recv[...], tmat[0, :, side], preferred_element_type=F32)
+        for d in range(1, SEQ):
+            kept = WIDTH - GROUP * d
+            conv[GROUP * d :, side] += jnp.dot(
+                m_recv[:kept, :], tmat[d, :, side], preferred_element_type=F32
+            )
+        if h == 0:
+            wait_bytes(q_recv.at[pl.ds(0, GROUP * (SEQ - 1)), :], a2a_sem.at[2])
+        g_send[h] = (q_recv[:, side].astype(F32) * (conv[:, side] + skip[:, side])).astype(BF)
 
     def land(yr):
         return pl.ds(aligned(yr * 2 * WIDTH + core * WIDTH + s * GROUP, GROUP), GROUP)
 
     for h in range(2):
+        gate(h)
         targets = same_core if h == RELAYED else sharing
         for p in (*peers[:5], None, *peers[5:]):
             rows = mine if p is None else pl.ds(aligned(p * GROUP, GROUP), GROUP)

time: 30.6 us -> 30.6 us (level)
  no operation moved by 1% of the time
where the time goes in v6:
time: 30.6 us; the launch traced here: 30.5 us
  Pallas kernels  29.8 us (97%)
  local copies, waits for them, and re-layouts  0.63 us (2%)
    pallas_call x1, Pallas kernels, body(): pl.pallas_call(kernel, out_shape=jax.ShapeDtypeStruct((ROWS, WIDTH), BF),...  29.8 us
    unnamed x1, local copies, waits for them, and re-layouts  0.63 us

profile of v6, /device:TPU:1, one launch (start us, length us, event | category | flops | bytes accessed | tf_op | source)
XLA Modules:
  0.0 30.5 jit_solution(5943583679081208282)
XLA Ops:
  0.0 29.8 %shard_map.64 = bf16[256,128]{1,0:T(8,128)(2,1)S(1)} custom-call(bf16[256,128]{1,0:T(8,128)(2,1)} %q_hbm.1, bf16[256,128]{1,0:T(8,128)(2,1)} %k_hbm.1, bf16[256,128]{1,0:T(8,128)(2,1)} %v_hbm.1, bf16[8,256]{1,0:T(8,128)(2,1)} %taps_hbm.1, f32[1,128]{1,0:T(1,128)} %bitcast.1, bf16[128,4096]{1,0:T(8,128)(2,1)} %w_hbm.1), custom_call_target="tpu_custom_call" | custom-call | tf_op jit(solution)/shard_map/pallas_call | solution.py:340
  29.8 0.6 %copy.8 = bf16[256,128]{1,0:T(8,128)(2,1)} copy(bf16[256,128]{1,0:T(8,128)(2,1)S(1)} %shard_map.64) | data formatting | bytes 131072

commit v7 on v5

--- a/solution.py
+++ b/solution.py
@@ -100,21 +100,11 @@
     flat_blocks = [(yh, r) for r in SHALLOW[:2]] + [(1 - yh, r) for r in SHALLOW[:2]]
     flat_blocks += [(yh, SHALLOW[2]), (1 - yh, SHALLOW[2])]
 
-    for n, group in enumerate(DEEP):
-        for r in group:
-            pltpu.make_async_copy(w_block(yh, r, core), deep_slot(r, 0), w_near.at[n]).start()
-    for n, (y, r) in enumerate(flat_blocks):
-        pltpu.make_async_copy(w_block(y, r, core), flat_slot(n), w_near.at[3]).start()
-
     loads[0].wait()
     loads[1].wait()
     mixed = (k_in[...].astype(F32) * v_in[...].astype(F32)).astype(BF)
     m_send[...] = mixed.astype(F32).T.astype(BF)
-    loads[2].wait()
-    q_send[...] = q_in[...].astype(F32).T.astype(BF)
     mine = pl.ds(aligned(s * GROUP, GROUP), GROUP)
-    m_recv[mine, :] = m_send[mine, :]
-    q_recv[mine, :] = q_send[mine, :]
     loads[3].wait()
     loads[4].wait()
     for n in range(SEQ):
@@ -128,6 +118,8 @@
     for p in peers:
         rows = pl.ds(aligned(p * GROUP, GROUP), GROUP)
         remote(m_send.at[rows, :], m_recv.at[mine, :], send_sem.at[1], a2a_sem.at[1], (p, k))
+    loads[2].wait()
+    q_send[...] = q_in[...].astype(F32).T.astype(BF)
     for p in peers:
         rows = pl.ds(aligned(p * GROUP, GROUP), GROUP)
         remote(q_send.at[rows, :], q_recv.at[mine, :], send_sem.at[2], a2a_sem.at[2], (p, k))
@@ -144,6 +136,14 @@
             remote(w_block(yh, r, 1 - core), deep_slot(r, 0), send_sem.at[3], w_far.at[n], (s, mate))
     for n, (y, r) in enumerate(flat_blocks):
         remote(w_block(y, r, 1 - core), flat_slot(n), send_sem.at[3], w_far.at[3], (s, mate))
+
+    m_recv[mine, :] = m_send[mine, :]
+    q_recv[mine, :] = q_send[mine, :]
+    for n, group in enumerate(DEEP):
+        for r in group:
+            pltpu.make_async_copy(w_block(yh, r, core), deep_slot(r, 0), w_near.at[n]).start()
+    for n, (y, r) in enumerate(flat_blocks):
+        pltpu.make_async_copy(w_block(y, r, core), flat_slot(n), w_near.at[3]).start()
 
     wait_bytes(taps_recv.at[pl.ds(0, SEQ - 1)], a2a_sem.at[0])
     row = lax.broadcasted_iota(jnp.int32, (ROWS, ROWS), 0)

time: 30.6 us -> 30.6 us (level)
  no operation moved by 1% of the time
where the time goes in v7:
time: 30.6 us; the launch traced here: 30.5 us
  Pallas kernels  29.9 us (98%)
  local copies, waits for them, and re-layouts  0.63 us (2%)
    pallas_call x1, Pallas kernels, body(): pl.pallas_call(kernel, out_shape=jax.ShapeDtypeStruct((ROWS, WIDTH), BF),...  29.9 us
    unnamed x1, local copies, waits for them, and re-layouts  0.63 us

profile of v7, /device:TPU:1, one launch (start us, length us, event | category | flops | bytes accessed | tf_op | source)
XLA Modules:
  0.0 30.5 jit_solution(3577936160426155213)
XLA Ops:
  0.0 29.9 %shard_map.64 = bf16[256,128]{1,0:T(8,128)(2,1)S(1)} custom-call(bf16[256,128]{1,0:T(8,128)(2,1)} %q_hbm.1, bf16[256,128]{1,0:T(8,128)(2,1)} %k_hbm.1, bf16[256,128]{1,0:T(8,128)(2,1)} %v_hbm.1, bf16[8,256]{1,0:T(8,128)(2,1)} %taps_hbm.1, f32[1,128]{1,0:T(1,128)} %bitcast.1, bf16[128,4096]{1,0:T(8,128)(2,1)} %w_hbm.1), custom_call_target="tpu_custom_call" | custom-call | tf_op jit(solution)/shard_map/pallas_call | solution.py:334
  29.9 0.6 %copy.8 = bf16[256,128]{1,0:T(8,128)(2,1)} copy(bf16[256,128]{1,0:T(8,128)(2,1)S(1)} %shard_map.64) | data formatting | bytes 131072
